TPU v7x, 128 devices: a whole 4x4x4 slice. The times are simulated.
128 devices in a mesh: band: 4 (over y), dom: 32 (over x, z, core).
Axes of the slice: x: 4, y: 4, z: 4, core: 2. Of those that a mesh axis runs over, the one named last changes fastest.
Arguments:
- orbitals: float32 [1024, 131072], P('band', 'dom'), may hold values from -6 to 6
- projectors: float32 [1024, 512, 128], P('dom'), may hold values from -0.25 to 0.25
- window_start: int32 [1024], P('dom'), may hold values from 0 to 3584
- slot_atom: int32 [32, 32], replicated, may hold values from 0 to 95, as said below
- atom_home: int32 [96], replicated, may hold values from 0 to 95, as said below
- atom_matrices: float32 [96, 128, 128], P('dom'), may hold values from -0.1875 to 0.1875
- rotation: float32 [1024, 1024], P('band'), may hold values from -0.1875 to 0.1875
Outputs:
- rotated: float32 [1024, 131072], P('band', 'dom')
Inputs may be any that keep to these rules, and one draw needn't show every extreme that they name: `atom_home`: a permutation; atom a is owned by domain atom_home[a] // 3, so every domain owns 3 atoms. `slot_atom`: in one domain at most 2 windows have atoms of one owner; in every domain some owner has exactly 2 of them, and some owner has exactly 2 from every domain.
All inputs are finite; a program needn't handle non-finite values.
Results may differ from a plain program's by a relative error of at most 0.0003.
Values sent between devices are 32-bit elements; how exact they have to be, the bound alone decides.
A program may use at most 128 MiB of HBM per device.

v0:
```python
import jax
import jax.numpy as jnp
from jax import lax
from jax.sharding import PartitionSpec as P

HIGHEST = lax.Precision.HIGHEST


def per_device(orbitals, projectors, window_start, slot_atom, atom_home, atom_matrices, rotation):
    own_domain = lax.axis_index("dom")
    slot_count = projectors.shape[0]
    window = projectors.shape[1]
    atom_count = atom_home.shape[0]
    windows = jax.vmap(lambda offset: lax.dynamic_slice_in_dim(orbitals, offset, window, 1))(
        window_start
    )
    partials = jnp.einsum("sbw,swp->sbp", windows, projectors, precision=HIGHEST)
    atom_ids = jnp.arange(atom_count, dtype=jnp.int32)
    home_table = jnp.sum(
        jnp.where(slot_atom[:, :, None] == atom_ids[None, None, :], atom_home[None, None, :], 0),
        axis=2,
    )
    own_home = lax.dynamic_index_in_dim(home_table, own_domain, 0, keepdims=False)
    home_match = (atom_ids[:, None] == own_home[None, :]).astype(jnp.float32)
    per_atom = jnp.einsum("rs,sbp->rbp", home_match, partials, precision=HIGHEST)
    owned_sums = lax.psum_scatter(per_atom, "dom", scatter_dimension=0, tiled=True)
    owned_factors = jnp.einsum("abp,apq->abq", owned_sums, atom_matrices, precision=HIGHEST)
    all_factors = lax.all_gather(owned_factors, "dom", axis=0, tiled=True)
    slot_factors = jnp.einsum("rs,rbp->sbp", home_match, all_factors, precision=HIGHEST)
    updates = jnp.einsum("sbq,swq->sbw", slot_factors, projectors, precision=HIGHEST)

    def add_window(slot_index, current):
        offset = window_start[slot_index]
        previous = lax.dynamic_slice_in_dim(current, offset, window, 1)
        return lax.dynamic_update_slice_in_dim(current, previous + updates[slot_index], offset, 1)

    corrected = lax.fori_loop(0, slot_count, add_window, orbitals)
    return jnp.dot(
        rotation,
        lax.all_gather(corrected, "band", axis=0, tiled=True),
        precision=HIGHEST,
        preferred_element_type=jnp.float32,
    )


def solution(mesh):
    in_specs = (
        P("band", "dom"),
        P("dom", None, None),
        P("dom"),
        P(),
        P(),
        P("dom", None, None),
        P("band", None),
    )
    out_specs = P("band", "dom")
    return jax.shard_map(
        per_device, mesh=mesh, in_specs=in_specs, out_specs=out_specs, check_vma=False
    )
```

profile of v0, /device:TPU:1, one launch (start us, length us, event | category | flops | bytes accessed | tf_op | source)
XLA Modules:
  0.0 820.3 jit_solution(12491529230231990169)
XLA Ops:
  6.6 4.7 copy.41
  11.3 107.9 %while.15 = (s32[]{:T(128)}, f32[256,4096]{1,0:T(8,128)}, s32[32,2]{0,1:T(2,128)S(1)}, f32[32,256,512]{2,1,0:T(8,128)}, s32[]{:T(128)}) while((s32[]{:T(128)}, f32[256,4096]{1,0:T(8,128)}, s32[32,2]{0,1:T(2,128)S(1)}, f32[32,256,512]{2,1,0:T(8,128)}, s32[]{:T(128)}) %tuple.39), condition=%wide.while_cond, body=%wide.while_body.sunk | while | flops 2 | bytes 1049689 | solution.py:14
  120.1 19.3 %fusion.12 = f32[32,256,128]{2,1,0:T(8,128)S(1)} fusion(f32[32,256,512]{2,1,0:T(8,128)} %get-tuple-element.92, f32[32,512,128]{2,1,0:T(8,128)} %param.10), kind=kOutput, calls=%fused_computation.19 | convolution fusion | flops 6442450944 | bytes 29360128 | tf_op jit(solution)/shard_map/sbw,swp->sbp/dot_general | solution.py:17
  139.3 11.5 %fusion.4 = f32[96,256,128]{2,0,1:T(8,128)} fusion(f32[32,256,128]{2,1,0:T(8,128)S(1)} %fusion.12, s32[32]{0:T(128)S(1)} %dynamic-slice_bitcast_fusion), kind=kOutput, calls=%fused_computation.8 | convolution fusion | flops 1207962624 | bytes 16777344 | tf_op jit(solution)/shard_map/rs,sbp->rbp/dot_general | solution.py:25
  150.8 16.4 %copy.16 = f32[96,256,128]{2,1,0:T(8,128)} copy(f32[96,256,128]{2,0,1:T(8,128)} %fusion.4) | data formatting | bytes 25165824 | tf_op jit(solution)/shard_map/rs,sbp->rbp/dot_general | solution.py:25
  167.2 106.7 %reduce-scatter.2.cloned.1.call-done = f32[3,256,128]{2,1,0:T(8,128)} async-done(((f32[96,256,128]{2,1,0:T(8,128)}), f32[3,256,128]{2,1,0:T(8,128)}) %reduce-scatter.2.cloned.1.call-update) | async-done | bytes 393232 | tf_op jit(solution)/shard_map/reduce_scatter | solution.py:26
  276.2 63.9 %all-gather.3.cloned.1.call-done = f32[96,256,128]{2,1,0:T(8,128)} async-done(((f32[3,256,128]{2,1,0:T(8,128)}), f32[96,256,128]{2,1,0:T(8,128)}) %all-gather.3.cloned.1.call-update) | async-done | bytes 12582928 | tf_op jit(solution)/shard_map/all_gather | solution.py:28
  340.1 16.1 %fusion = f32[32,256,128]{2,0,1:T(8,128)S(1)} fusion(f32[96,256,128]{2,1,0:T(8,128)} %all-gather.3.cloned.1.call-done, s32[32]{0:T(128)S(1)} %dynamic-slice_bitcast_fusion), kind=kOutput, calls=%fused_computation.3 | convolution fusion | flops 1207962624 | bytes 16777344 | tf_op jit(solution)/shard_map/rs,rbp->sbp/dot_general | solution.py:29
  356.3 20.9 %fusion.2 = f32[32,256,512]{2,1,0:T(8,128)} fusion(f32[32,512,128]{2,1,0:T(8,128)} %param.10, f32[32,256,128]{2,0,1:T(8,128)S(1)} %fusion), kind=kOutput, calls=%fused_computation.6 | convolution fusion | flops 6442450944 | bytes 29360128 | tf_op jit(solution)/shard_map/sbq,swq->sbw/dot_general | solution.py:30
  377.2 246.7 %while.14 = (s32[]{:T(128)}, f32[256,4096]{1,0:T(8,128)}, s32[32]{0:T(128)S(1)}, f32[32,256,512]{2,1,0:T(8,128)}, s32[]{:T(128)}, /*index=5*/s32[]{:T(128)}, s32[]{:T(128)}) while((s32[]{:T(128)}, f32[256,4096]{1,0:T(8,128)}, s32[32]{0:T(128)S(1)}, f32[32,256,512]{2,1,0:T(8,128)}, s32[]{:T(128)}, /*index=5*/s32[]{:T(128)}, s32[]{:T(128)}) %tuple.52), condition=%wide.region_3.4_spmd, body=%wide.region_2.3_spmd.sunk | while | flops 131077 | bytes 2621575 | solution.py:37
  388.8 3.8 dynamic_update_slice.8
  396.5 3.8 dynamic_update_slice.8
  412.0 3.8 dynamic_update_slice.8
  419.7 3.8 dynamic_update_slice.8
  427.4 3.8 dynamic_update_slice.8
  435.1 3.8 dynamic_update_slice.8
  442.9 3.8 dynamic_update_slice.8
  450.6 3.8 dynamic_update_slice.8
  458.3 3.8 dynamic_update_slice.8
  466.1 3.8 dynamic_update_slice.8
  473.8 3.8 dynamic_update_slice.8
  481.5 3.8 dynamic_update_slice.8
  489.2 3.8 dynamic_update_slice.8
  497.0 3.8 dynamic_update_slice.8
  504.7 3.8 dynamic_update_slice.8
  512.4 3.8 dynamic_update_slice.8
  520.2 3.8 dynamic_update_slice.8
  543.4 3.8 dynamic_update_slice.8
  612.5 3.8 dynamic_update_slice.8
  624.0 153.9 %all-gather.5.cloned.1.call-done = f32[1024,4096]{1,0:T(8,128)} async-done(((f32[256,4096]{1,0:T(8,128)}), f32[1024,4096]{1,0:T(8,128)}) %all-gather.5.cloned.1.call-update) | async-done | bytes 16777232 | tf_op jit(solution)/shard_map/all_gather | solution.py:40
  777.8 30.1 %convolution_bitcast_fusion = f32[256,4096]{0,1:T(8,128)} fusion(f32[1024,4096]{1,0:T(8,128)} %all-gather.5.cloned.1.call-done, f32[256,1024]{1,0:T(8,128)S(1)} %copy-done), kind=kOutput, calls=%fused_computation.5 | convolution fusion | flops 12884901888 | bytes 22020096 | tf_op jit(solution)/shard_map/dot_general | solution.py:38
  807.9 5.6 copy.19
  (195 shorter events, 225.2 us)
Async XLA Ops:
  6.5 771.3 %copy-start = (f32[256,1024]{1,0:T(8,128)S(1)}, f32[256,1024]{1,0:T(8,128)}, u32[]{:S(2)}) copy-start(f32[256,1024]{1,0:T(8,128)} %param.15) | copy-start | bytes 3145732
  6.5 4.8 copy-start.4
  6.5 112.7 %copy-start.2 = (s32[32,32]{1,0:T(8,128)S(1)}, s32[32,32]{1,0:T(8,128)}, u32[]{:S(2)}) copy-start(s32[32,32]{1,0:T(8,128)} %param.12) | copy-start | bytes 12292
  6.5 112.7 %copy-start.3 = (s32[96]{0:T(128)S(1)}, s32[96]{0:T(128)}, u32[]{:S(2)}) copy-start(s32[96]{0:T(128)} %param.13) | copy-start | bytes 1156
  6.5 267.4 %reduce-scatter.2.cloned.1.call-start = ((), (), s32[]{:S(2)}) async-start(), calls=%async_computation.1 | async-start | bytes 12976128 | tf_op jit(solution)/shard_map/reduce_scatter | solution.py:26
  167.2 106.7 %copy-start.1 = (f32[3,128,128]{2,1,0:T(8,128)S(1)}, f32[3,128,128]{2,1,0:T(8,128)}, u32[]{:S(2)}) copy-start(f32[3,128,128]{2,1,0:T(8,128)} %param.14) | copy-start | bytes 589828
  167.2 172.9 %all-gather.3.cloned.1.call-start = ((), (), s32[]{:S(2)}) async-start(), calls=%async_computation.2 | async-start | bytes 12976128 | tf_op jit(solution)/shard_map/all_gather | solution.py:28
  276.2 501.7 %all-gather.5.cloned.1.call-start = ((), (), s32[]{:S(2)}) async-start(), calls=%async_computation.3 | async-start | bytes 20971520 | tf_op jit(solution)/shard_map/all_gather | solution.py:40
Sparse Core Ops, SparseCore 0:
  167.3 106.5 reduce-scatter.1
  276.4 63.6 all-gather.2
  624.1 153.7 all-gather.4
where the time goes:
time: 834 us; the launch traced here: 820 us
  waiting for transfers between devices  324 us (39%)
  local copies, waits for them, and re-layouts  273 us (33%)
  matrix products  100 us (12%)
  loops' own time  61.3 us (7%)
  other arithmetic  47.4 us (6%)
  between operations  13.4 us (2%)
    all_gather x1, waiting for transfers between devices, per_device(): lax.all_gather(corrected, 'band', axis=0, tiled=True)  154 us
    dynamic_update_slice x32, local copies, waits for them, and re-layouts, add_window(): lax.dynamic_update_slice_in_dim(current, previous + updates[slot_index],...  120 us
    gather x96, local copies, waits for them, and re-layouts  108 us
    reduce_scatter x1, waiting for transfers between devices, per_device(): lax.psum_scatter(per_atom, 'dom', scatter_dimension=0, tiled=True)  107 us
    all_gather x1, waiting for transfers between devices, per_device(): all_factors = lax.all_gather(owned_factors, 'dom', axis=0, tiled=True)  63.9 us
    another operation x1, loops' own time, per_device(): corrected = lax.fori_loop(0, slot_count, add_window, orbitals)  61.3 us
    add x32, other arithmetic, add_window(): previous + updates[slot_index]  46.6 us
    dot_general x1, matrix products, per_device(): jnp.dot(rotation, lax.all_gather(corrected, 'band', axis=0, tiled=True),...  30.1 us
  transfers between devices with their start and end apart: 3, of which 3 were waited for; matrix products, arithmetic and copies ran while one was open for 0% of the time, Pallas kernels for 0%

commit v1 on v0

--- a/solution.py
+++ b/solution.py
@@ -25,7 +25,9 @@
     per_atom = jnp.einsum("rs,sbp->rbp", home_match, partials, precision=HIGHEST)
     owned_sums = lax.psum_scatter(per_atom, "dom", scatter_dimension=0, tiled=True)
     owned_factors = jnp.einsum("abp,apq->abq", owned_sums, atom_matrices, precision=HIGHEST)
-    all_factors = lax.all_gather(owned_factors, "dom", axis=0, tiled=True)
+    all_factors = jnp.concatenate(
+        lax.all_to_all(jnp.stack([owned_factors] * lax.axis_size("dom")), "dom", 0, 0), axis=0
+    )
     slot_factors = jnp.einsum("rs,rbp->sbp", home_match, all_factors, precision=HIGHEST)
     updates = jnp.einsum("sbq,swq->sbw", slot_factors, projectors, precision=HIGHEST)
 

time: 834 us -> 977 us (1.17)
  waiting for transfers between devices: 324 us -> 459 us
    all_to_all x0 -> x1, waiting for transfers between devices: none -> 175 us  [per_device(): lax.all_to_all(jnp.stack([owned_factors] * lax.axis_size('dom')), 'dom',...]
    all_gather x1 -> x0, waiting for transfers between devices: 63.9 us -> none  [per_device(): all_factors = lax.all_gather(owned_factors, 'dom', axis=0, tiled=True)]
    all_gather x1, waiting for transfers between devices: 154 us -> 177 us  [per_device(): lax.all_gather(corrected, 'band', axis=0, tiled=True)]
where the time goes in v1:
time: 977 us; the launch traced here: 964 us
  waiting for transfers between devices  459 us (47%)
  local copies, waits for them, and re-layouts  278 us (28%)
  matrix products  99.3 us (10%)
  loops' own time  60.2 us (6%)
  other arithmetic  47.4 us (5%)
  between operations  13.7 us (1%)
    all_gather x1, waiting for transfers between devices, per_device(): lax.all_gather(corrected, 'band', axis=0, tiled=True)  177 us
    all_to_all x1, waiting for transfers between devices, per_device(): lax.all_to_all(jnp.stack([owned_factors] * lax.axis_size('dom')), 'dom',...  175 us
    dynamic_update_slice x32, local copies, waits for them, and re-layouts, add_window(): lax.dynamic_update_slice_in_dim(current, previous + updates[slot_index],...  120 us
    reduce_scatter x1, waiting for transfers between devices, per_device(): lax.psum_scatter(per_atom, 'dom', scatter_dimension=0, tiled=True)  107 us
    gather x96, local copies, waits for them, and re-layouts  106 us
    another operation x1, loops' own time, per_device(): corrected = lax.fori_loop(0, slot_count, add_window, orbitals)  60.2 us
    add x32, other arithmetic, add_window(): previous + updates[slot_index]  46.6 us
    dot_general x1, matrix products, per_device(): jnp.dot(rotation, lax.all_gather(corrected, 'band', axis=0, tiled=True),...  30.1 us
  transfers between devices with their start and end apart: 3, of which 3 were waited for; matrix products, arithmetic and copies ran while one was open for 0% of the time, Pallas kernels for 0%

profile of v1, /device:TPU:1, one launch (start us, length us, event | category | flops | bytes accessed | tf_op | source)
XLA Modules:
  0.0 963.6 jit_solution(8386886533152947112)
XLA Ops:
  6.6 4.7 copy.35
  11.3 106.3 %while.15 = (s32[]{:T(128)}, f32[256,4096]{1,0:T(8,128)}, s32[32,2]{0,1:T(2,128)S(1)}, f32[32,256,512]{2,1,0:T(8,128)}, s32[]{:T(128)}) while((s32[]{:T(128)}, f32[256,4096]{1,0:T(8,128)}, s32[32,2]{0,1:T(2,128)S(1)}, f32[32,256,512]{2,1,0:T(8,128)}, s32[]{:T(128)}) %tuple.39), condition=%wide.while_cond, body=%wide.while_body.sunk | while | flops 2 | bytes 1049689 | solution.py:14
  118.5 19.3 %fusion.12 = f32[32,256,128]{2,1,0:T(8,128)S(1)} fusion(f32[32,256,512]{2,1,0:T(8,128)} %get-tuple-element.92, f32[32,512,128]{2,1,0:T(8,128)} %param.10), kind=kOutput, calls=%fused_computation.19 | convolution fusion | flops 6442450944 | bytes 29360128 | tf_op jit(solution)/shard_map/sbw,swp->sbp/dot_general | solution.py:17
  137.7 11.5 %fusion.4 = f32[96,256,128]{2,0,1:T(8,128)} fusion(f32[32,256,128]{2,1,0:T(8,128)S(1)} %fusion.12, s32[32]{0:T(128)S(1)} %dynamic-slice_bitcast_fusion), kind=kOutput, calls=%fused_computation.8 | convolution fusion | flops 1207962624 | bytes 16777344 | tf_op jit(solution)/shard_map/rs,sbp->rbp/dot_general | solution.py:25
  149.2 16.4 %copy.11 = f32[96,256,128]{2,1,0:T(8,128)} copy(f32[96,256,128]{2,0,1:T(8,128)} %fusion.4) | data formatting | bytes 25165824 | tf_op jit(solution)/shard_map/rs,sbp->rbp/dot_general | solution.py:25
  165.6 106.7 %reduce-scatter.2.cloned.1.call-done = f32[3,256,128]{2,1,0:T(8,128)} async-done(((f32[96,256,128]{2,1,0:T(8,128)}), f32[3,256,128]{2,1,0:T(8,128)}) %reduce-scatter.2.cloned.1.call-update) | async-done | bytes 393232 | tf_op jit(solution)/shard_map/reduce_scatter | solution.py:26
  273.8 6.0 stack.2
  279.9 6.7 all-to-all-start
  286.7 174.6 %all-to-all-done = f32[32,3,256,128]{3,2,1,0:T(8,128)} async-done(((f32[32,3,256,128]{3,2,1,0:T(8,128)}), f32[32,3,256,128]{3,2,1,0:T(8,128)}, u32[]{:S(2)}, u32[]{:S(2)}) %all-to-all-start) | async-done | bytes 12582944 | tf_op jit(solution)/shard_map/all_to_all | solution.py:29
  461.3 16.1 %fusion = f32[32,256,128]{2,0,1:T(8,128)S(1)} fusion(f32[96,256,128]{2,1,0:T(8,128)} %bitcast.5, s32[32]{0:T(128)S(1)} %dynamic-slice_bitcast_fusion), kind=kOutput, calls=%fused_computation.3 | convolution fusion | flops 1207962624 | bytes 16777344 | tf_op jit(solution)/shard_map/rs,rbp->sbp/dot_general | solution.py:31
  477.4 21.0 %fusion.2 = f32[32,256,512]{2,1,0:T(8,128)} fusion(f32[32,512,128]{2,1,0:T(8,128)} %param.10, f32[32,256,128]{2,0,1:T(8,128)S(1)} %fusion), kind=kOutput, calls=%fused_computation.6 | convolution fusion | flops 6442450944 | bytes 29360128 | tf_op jit(solution)/shard_map/sbq,swq->sbw/dot_general | solution.py:32
  498.3 245.3 %while.14 = (s32[]{:T(128)}, f32[256,4096]{1,0:T(8,128)}, s32[32]{0:T(128)S(1)}, f32[32,256,512]{2,1,0:T(8,128)}, s32[]{:T(128)}, /*index=5*/s32[]{:T(128)}, s32[]{:T(128)}) while((s32[]{:T(128)}, f32[256,4096]{1,0:T(8,128)}, s32[32]{0:T(128)S(1)}, f32[32,256,512]{2,1,0:T(8,128)}, s32[]{:T(128)}, /*index=5*/s32[]{:T(128)}, s32[]{:T(128)}) %tuple.50), condition=%wide.region_3.4_spmd, body=%wide.region_2.3_spmd.sunk | while | flops 131077 | bytes 2621575 | solution.py:39
  509.8 3.8 dynamic_update_slice.8
  517.5 3.8 dynamic_update_slice.8
  532.8 3.8 dynamic_update_slice.8
  540.5 3.8 dynamic_update_slice.8
  548.2 3.8 dynamic_update_slice.8
  555.9 3.8 dynamic_update_slice.8
  563.6 3.8 dynamic_update_slice.8
  571.2 3.8 dynamic_update_slice.8
  578.9 3.8 dynamic_update_slice.8
  586.6 3.8 dynamic_update_slice.8
  594.3 3.8 dynamic_update_slice.8
  602.0 3.8 dynamic_update_slice.8
  609.7 3.8 dynamic_update_slice.8
  617.3 3.8 dynamic_update_slice.8
  625.0 3.8 dynamic_update_slice.8
  732.1 3.8 dynamic_update_slice.8
  739.8 3.8 dynamic_update_slice.8
  743.6 177.3 %all-gather.2.cloned.1.call-done = f32[1024,4096]{1,0:T(8,128)} async-done(((f32[256,4096]{1,0:T(8,128)}), f32[1024,4096]{1,0:T(8,128)}) %all-gather.2.cloned.1.call-update) | async-done | bytes 16777232 | tf_op jit(solution)/shard_map/all_gather | solution.py:42
  920.9 30.1 %convolution_bitcast_fusion = f32[256,4096]{0,1:T(8,128)} fusion(f32[1024,4096]{1,0:T(8,128)} %all-gather.2.cloned.1.call-done, f32[256,1024]{1,0:T(8,128)S(1)} %copy-done), kind=kOutput, calls=%fused_computation.5 | convolution fusion | flops 12884901888 | bytes 22020096 | tf_op jit(solution)/shard_map/dot_general | solution.py:40
  951.0 5.6 copy.9
  (195 shorter events, 229.9 us)
Async XLA Ops:
  6.5 914.4 %copy-start = (f32[256,1024]{1,0:T(8,128)S(1)}, f32[256,1024]{1,0:T(8,128)}, u32[]{:S(2)}) copy-start(f32[256,1024]{1,0:T(8,128)} %param.15) | copy-start | bytes 3145732
  6.5 4.8 copy-start.4
  6.5 111.1 %copy-start.2 = (s32[32,32]{1,0:T(8,128)S(1)}, s32[32,32]{1,0:T(8,128)}, u32[]{:S(2)}) copy-start(s32[32,32]{1,0:T(8,128)} %param.12) | copy-start | bytes 12292
  6.5 111.1 %copy-start.3 = (s32[96]{0:T(128)S(1)}, s32[96]{0:T(128)}, u32[]{:S(2)}) copy-start(s32[96]{0:T(128)} %param.13) | copy-start | bytes 1156
  6.5 265.8 %reduce-scatter.2.cloned.1.call-start = ((), (), s32[]{:S(2)}) async-start(), calls=%async_computation.2 | async-start | bytes 12976128 | tf_op jit(solution)/shard_map/reduce_scatter | solution.py:26
  165.6 106.8 %copy-start.1 = (f32[3,128,128]{2,1,0:T(8,128)S(1)}, f32[3,128,128]{2,1,0:T(8,128)}, u32[]{:S(2)}) copy-start(f32[3,128,128]{2,1,0:T(8,128)} %param.14) | copy-start | bytes 589828
  279.9 181.4 %all-to-all-start = ((f32[32,3,256,128]{3,2,1,0:T(8,128)}), f32[32,3,256,128]{3,2,1,0:T(8,128)}, u32[]{:S(2)}, u32[]{:S(2)}) async-start(f32[32,3,256,128]{3,2,1,0:T(8,128)} %stack.2), calls=%async_computation.1 | async-start | bytes 25165824 | tf_op jit(solution)/shard_map/all_to_all | solution.py:29
  286.6 634.3 %all-gather.2.cloned.1.call-start = ((), (), s32[]{:S(2)}) async-start(), calls=%async_computation.3 | async-start | bytes 20971520 | tf_op jit(solution)/shard_map/all_gather | solution.py:42
Sparse Core Ops, SparseCore 0:
  165.7 106.5 reduce-scatter.1
  743.7 177.1 all-gather.1
